TPU v7x, 256 devices: a whole 4x4x8 slice. The times are simulated.
256 devices in a mesh: seq: 128 (over x_lo, y, z, core), head: 2 (over x_hi).
Axes of the slice: x: 4 (x_hi: 2, x_lo: 2; x = x_hi * 2 + x_lo), y: 4, z: 8, core: 2. Of those that a mesh axis runs over, the one named last changes fastest.
Arguments:
- query: bfloat16 [32768, 3584], P('seq', 'head'), may hold values from -6 to 6
- key: bfloat16 [32768, 512], P('seq', 'head'), may hold values from -6 to 6
- value: bfloat16 [32768, 512], P('seq', 'head'), may hold values from -6 to 6
- output: bfloat16 [32768, 3584], P('seq', 'head'), may hold values from -6 to 6
- output_gradient: bfloat16 [32768, 3584], P('seq', 'head'), may hold values from -6 to 6
- lse: float32 [28, 32768], P('head', 'seq'), may hold values from 3 to 6
- doc_lengths: int32 [32], replicated, may hold values from 1 to 2048, as said below
- w_query: bfloat16 [3584, 3584], P('seq', 'head'), may hold values from -0.09375 to 0.09375
- key_weight: bfloat16 [3584, 512], P('seq', 'head'), may hold values from -0.09375 to 0.09375
- value_weight: bfloat16 [3584, 512], P('seq', 'head'), may hold values from -0.09375 to 0.09375
Outputs:
- grad_input: bfloat16 [32768, 3584], P('seq', 'head')
Inputs may be any that keep to these rules, and one draw needn't show every extreme that they name: `doc_lengths`: the documents lie end to end and fill the 32768 tokens of the pack; the first has 1024 tokens, and one of exactly 2048 tokens begins at token 15360.
All inputs are finite; a program needn't handle non-finite values.
Results may differ from a plain program's by a relative error of at most 0.0056.
Values may be sent and summed in bfloat16 or wider, within the bound.
A program may use at most 128 MiB of HBM per device.

v0:
```python
import math
import jax
import jax.numpy as jnp
from jax import lax
from jax.sharding import PartitionSpec as P

HEAD_SIZE = 128
WINDOW = 512


def shifted(array, axis, by):
    peers = lax.axis_size(axis)
    pairs = [(i, i + by) for i in range(peers) if 0 <= i + by < peers]
    return lax.ppermute(array, axis, pairs)


def lower_bounds(positions, doc_lengths, window):
    starts = jnp.cumsum(doc_lengths, dtype=jnp.int32) - doc_lengths
    inside = starts[None, :] <= positions[:, None]
    doc_begin = jnp.max(jnp.where(inside, starts[None, :], 0), axis=1)
    return jnp.maximum(doc_begin, positions - window + 1)


def attend(
    query_rows,
    key_row_block,
    value_row_block,
    visible,
    logsumexp_rows,
    output_grad_rows,
    row_delta,
    score_scale,
):
    scores = (
        jnp.einsum("tgjd,kgd->gjtk", query_rows, key_row_block, preferred_element_type=jnp.float32)
        * score_scale
    )
    prob_full = jnp.where(visible[None, None], jnp.exp(scores - logsumexp_rows[..., None]), 0.0)
    prob_low = prob_full.astype(jnp.bfloat16)
    grad_val = jnp.einsum(
        "gjtk,tgjd->kgd", prob_low, output_grad_rows, preferred_element_type=jnp.float32
    )
    grad_prob = jnp.einsum(
        "tgjd,kgd->gjtk", output_grad_rows, value_row_block, preferred_element_type=jnp.float32
    )
    dscore = (prob_full * (grad_prob - row_delta[..., None]) * score_scale).astype(jnp.bfloat16)
    grad_qry = jnp.einsum(
        "gjtk,kgd->tgjd", dscore, key_row_block, preferred_element_type=jnp.float32
    )
    grad_key = jnp.einsum("gjtk,tgjd->kgd", dscore, query_rows, preferred_element_type=jnp.float32)
    return (grad_qry, grad_key, grad_val)


def projector(grad_rows, w_piece):
    return jnp.einsum("tc,rc->tr", grad_rows, w_piece, preferred_element_type=jnp.float32)


def shards(
    query, key, value, output, output_gradient, lse, doc_lengths, w_query, key_weight, value_weight
):
    tok_rows = query.shape[0]
    key_value_width = key.shape[1]
    kv_heads = key_value_width // HEAD_SIZE
    q_heads = query.shape[1] // HEAD_SIZE
    per_group = q_heads // kv_heads
    score_scale = 1.0 / math.sqrt(HEAD_SIZE)
    seq_index = lax.axis_index("seq")
    positions = seq_index * tok_rows + jnp.arange(tok_rows, dtype=jnp.int32)
    lower = lower_bounds(positions, doc_lengths, WINDOW)
    query_rows = query.reshape(tok_rows, kv_heads, per_group, HEAD_SIZE)
    output_rows = output.reshape(tok_rows, kv_heads, per_group, HEAD_SIZE)
    output_grad_rows = output_gradient.reshape(tok_rows, kv_heads, per_group, HEAD_SIZE)
    row_delta = jnp.einsum(
        "tgjd,tgjd->gjt", output_grad_rows, output_rows, preferred_element_type=jnp.float32
    )
    logsumexp_rows = lse.reshape(kv_heads, per_group, tok_rows)
    near_pair = shifted((key, value), "seq", 1)
    far_pair = shifted((key, value), "seq", 2)
    key_all = jnp.concatenate([far_pair[0], near_pair[0], key], 0).reshape(
        3 * tok_rows, kv_heads, HEAD_SIZE
    )
    value_all = jnp.concatenate([far_pair[1], near_pair[1], value], 0).reshape(
        3 * tok_rows, kv_heads, HEAD_SIZE
    )
    key_pos = positions[0] - 2 * tok_rows + jnp.arange(3 * tok_rows, dtype=jnp.int32)
    visible = (key_pos[None, :] >= lower[:, None]) & (key_pos[None, :] <= positions[:, None])
    grad_qry, grad_key, grad_val = attend(
        query_rows,
        key_all,
        value_all,
        visible,
        logsumexp_rows,
        output_grad_rows,
        row_delta,
        score_scale,
    )
    key_parts = grad_key.reshape(3, tok_rows, key_value_width)
    value_parts = grad_val.reshape(3, tok_rows, key_value_width)
    key_far, key_near, key_own = (key_parts[0], key_parts[1], key_parts[2])
    value_far, value_near, value_own = (value_parts[0], value_parts[1], value_parts[2])
    back_near = shifted((key_near, value_near), "seq", -1)
    back_far = shifted((key_far, value_far), "seq", -2)
    key_total = key_own + back_near[0] + back_far[0]
    value_total = value_own + back_near[1] + back_far[1]
    q_grad_low = grad_qry.reshape(tok_rows, q_heads * HEAD_SIZE).astype(jnp.bfloat16)
    k_grad_low = key_total.astype(jnp.bfloat16)
    v_grad_low = value_total.astype(jnp.bfloat16)
    partial_sum = projector(q_grad_low, lax.all_gather(w_query, "seq", axis=0, tiled=True))
    partial_sum = partial_sum + projector(
        k_grad_low, lax.all_gather(key_weight, "seq", axis=0, tiled=True)
    )
    partial_sum = partial_sum + projector(
        v_grad_low, lax.all_gather(value_weight, "seq", axis=0, tiled=True)
    )
    summed = lax.psum_scatter(partial_sum, "head", scatter_dimension=1, tiled=True)
    return summed.astype(jnp.bfloat16)


def solution(mesh):
    in_specs = (
        P("seq", "head"),
        P("seq", "head"),
        P("seq", "head"),
        P("seq", "head"),
        P("seq", "head"),
        P("head", "seq"),
        P(),
        P("seq", "head"),
        P("seq", "head"),
        P("seq", "head"),
    )
    out_specs = P("seq", "head")
    return jax.shard_map(shards, mesh=mesh, in_specs=in_specs, out_specs=out_specs, check_vma=False)
```

profile of v0, /device:TPU:1, one launch (start us, length us, event | category | flops | bytes accessed | tf_op | source)
XLA Modules:
  0.0 768.8 jit_solution(6138011124968313008)
XLA Ops:
  6.5 0.7 all-gather.9.cloned.1.call-update
  7.3 0.7 all-gather.11.cloned.1.call-update
  8.1 0.7 all-gather.7.cloned.1.call-update
  8.8 1.0 copy.61
  9.8 4.9 collective-permute-start.3
  14.7 3.5 collective-permute-start.2
  18.3 1.0 copy.54
  19.3 2.2 collective-permute-start.1
  21.5 3.5 collective-permute-start
  25.1 0.6 copy-done.1
  25.6 0.5 slice.27
  26.2 0.7 sub.31
  26.9 0.7 copy.57
  27.7 0.1 reduce.1
  27.8 1.2 sub.30
  29.0 1.5 copy.64
  30.5 1.5 copy.58
  32.0 1.5 copy.93
  34.1 0.8 select_reduce_fusion
  34.9 0.9 compare_and_fusion
  35.8 0.3 fusion.9
  36.1 1.6 fusion.21
  37.7 2.4 fusion.10
  40.2 0.1 fusion.19
  40.3 1.3 collective-permute-start.7
  41.6 2.4 collective-permute-start.6
  44.0 4.0 fusion.2
  48.0 1.9 convolution_bitcast_fusion
  49.9 0.1 fusion.20
  50.0 1.3 collective-permute-start.5
  51.3 2.1 collective-permute-start.4
  53.4 0.9 convolution_convert_fusion
  54.3 0.6 collective-permute-done.6
  55.0 7.5 collective-permute-done.5
  62.5 2.8 collective-permute-done.4
  65.3 0.1 fusion.16
  65.3 172.2 %all-gather.9.cloned.1.call-done = bf16[128,28,256]{2,1,0:T(8,128)(2,1)} async-done(((bf16[1,28,256]{2,1,0:T(8,128)(2,1)}), bf16[128,28,256]{2,1,0:T(8,128)(2,1)}) %all-gather.9.cloned.1.call-update) | async-done | bytes 1835024 | tf_op jit(solution)/shard_map/all_gather | solution.py:110
  237.5 2.5 reshape.141
  240.0 210.2 %all-gather.11.cloned.1.call-done = bf16[128,28,256]{2,1,0:T(8,128)(2,1)} async-done(((bf16[1,28,256]{2,1,0:T(8,128)(2,1)}), bf16[128,28,256]{2,1,0:T(8,128)(2,1)}) %all-gather.11.cloned.1.call-update) | async-done | bytes 1835024 | tf_op jit(solution)/shard_map/all_gather | solution.py:113
  450.1 3.8 reshape.143
  453.9 222.8 %all-gather.7.cloned.1.call-done = bf16[128,28,1792]{2,1,0:T(8,128)(2,1)} async-done(((bf16[1,28,1792]{2,1,0:T(8,128)(2,1)}), bf16[128,28,1792]{2,1,0:T(8,128)(2,1)}) %all-gather.7.cloned.1.call-update) | async-done | bytes 12845072 | tf_op jit(solution)/shard_map/all_gather | solution.py:108
  676.7 17.6 %reshape.139 = bf16[3584,1792]{1,0:T(8,128)(2,1)} reshape(bf16[128,28,1792]{2,1,0:T(8,128)(2,1)} %all-gather.7.cloned.1.call-done) | data formatting | bytes 25690112
  694.3 6.6 fusion.22
  701.0 0.7 convolution_add_fusion.1
  701.7 0.8 copy-done
  702.5 2.5 convolution_add_fusion
  705.0 54.7 %reduce-scatter.2.cloned.1.call-done = f32[256,1792]{1,0:T(8,128)} async-done(((f32[256,3584]{1,0:T(8,128)}), f32[256,1792]{1,0:T(8,128)}) %reduce-scatter.2.cloned.1.call-update) | async-done | bytes 1835024 | tf_op jit(solution)/shard_map/reduce_scatter | solution.py:115
  759.7 2.5 convert_element_type.31
  (19 shorter events, 0.3 us)
Async XLA Ops:
  6.5 231.0 %all-gather.9.cloned.1.call-start = ((), (), s32[]{:S(2)}) async-start(), calls=%async_computation.3 | async-start | bytes 2113536 | tf_op jit(solution)/shard_map/all_gather | solution.py:110
  7.3 442.9 %all-gather.11.cloned.1.call-start = ((), (), s32[]{:S(2)}) async-start(), calls=%async_computation.4 | async-start | bytes 2113536 | tf_op jit(solution)/shard_map/all_gather | solution.py:113
  8.0 668.7 %all-gather.7.cloned.1.call-start = ((), (), s32[]{:S(2)}) async-start(), calls=%async_computation.2 | async-start | bytes 14794752 | tf_op jit(solution)/shard_map/all_gather | solution.py:108
  8.7 751.0 %reduce-scatter.2.cloned.1.call-start = ((), (), s32[]{:S(2)}) async-start(), calls=%async_computation.1 | async-start | bytes 5505024 | tf_op jit(solution)/shard_map/reduce_scatter | solution.py:115
  9.8 34.2 %collective-permute-start.3 = (bf16[256,256]{0,1:T(8,128)(2,1)S(1)}, bf16[256,256]{0,1:T(8,128)(2,1)S(1)}, u32[]{:S(2)}, u32[]{:S(2)}) collective-permute-start(bf16[256,256]{0,1:T(8,128)(2,1)S(1)} %copy.61), channel_id=1, source_target_pairs={{0,2},{2,4},{4,6},{6,8},{8,10},{10,12},{12,14},{14,16},{16,18},{18... | collective-permute-start | bytes 393224 | tf_op jit(solution)/shard_map/ppermute | solution.py:14
  14.7 29.3 %collective-permute-start.2 = (bf16[256,256]{0,1:T(8,128)(2,1)S(1)}, bf16[256,256]{0,1:T(8,128)(2,1)S(1)}, u32[]{:S(2)}, u32[]{:S(2)}) collective-permute-start(bf16[256,256]{0,1:T(8,128)(2,1)S(1)} %copy.61), channel_id=1, source_target_pairs={{0,4},{2,6},{4,8},{6,10},{8,12},{10,14},{12,16},{14,18},{16,20},{1... | collective-permute-start | bytes 393224 | tf_op jit(solution)/shard_map/ppermute | solution.py:14
  19.3 16.8 %collective-permute-start.1 = (bf16[256,256]{0,1:T(8,128)(2,1)S(1)}, bf16[256,256]{0,1:T(8,128)(2,1)S(1)}, u32[]{:S(2)}, u32[]{:S(2)}) collective-permute-start(bf16[256,256]{0,1:T(8,128)(2,1)S(1)} %copy.54), channel_id=1, source_target_pairs={{0,2},{2,4},{4,6},{6,8},{8,10},{10,12},{12,14},{14,16},{16,18},{18... | collective-permute-start | bytes 393224 | tf_op jit(solution)/shard_map/ppermute | solution.py:14
  21.5 14.6 %collective-permute-start = (bf16[256,256]{0,1:T(8,128)(2,1)S(1)}, bf16[256,256]{0,1:T(8,128)(2,1)S(1)}, u32[]{:S(2)}, u32[]{:S(2)}) collective-permute-start(bf16[256,256]{0,1:T(8,128)(2,1)S(1)} %copy.54), channel_id=1, source_target_pairs={{0,4},{2,6},{4,8},{6,10},{8,12},{10,14},{12,16},{14,18},{16,20},{1... | collective-permute-start | bytes 393224 | tf_op jit(solution)/shard_map/ppermute | solution.py:14
  25.1 0.6 copy-start.1
  40.3 14.0 %collective-permute-start.7 = (f32[256,256]{0,1:T(8,128)S(1)}, f32[256,256]{0,1:T(8,128)S(1)}, u32[]{:S(2)}, u32[]{:S(2)}) collective-permute-start(f32[256,256]{0,1:T(8,128)S(1)} %bitcast.104), channel_id=1, source_target_pairs={{4,0},{6,2},{8,4},{10,6},{12,8},{14,10},{16,12},{18,14},{20,16},{2... | collective-permute-start | bytes 786440 | tf_op jit(solution)/shard_map/ppermute | solution.py:14
  41.6 13.4 %collective-permute-start.6 = (f32[256,256]{0,1:T(8,128)S(1)}, f32[256,256]{0,1:T(8,128)S(1)}, u32[]{:S(2)}, u32[]{:S(2)}) collective-permute-start(f32[256,256]{0,1:T(8,128)S(1)} %bitcast.103), channel_id=1, source_target_pairs={{2,0},{4,2},{6,4},{8,6},{10,8},{12,10},{14,12},{16,14},{18,16},{20... | collective-permute-start | bytes 786440 | tf_op jit(solution)/shard_map/ppermute | solution.py:14
  50.0 12.5 %collective-permute-start.5 = (f32[256,256]{0,1:T(8,128)S(1)}, f32[256,256]{0,1:T(8,128)S(1)}, u32[]{:S(2)}, u32[]{:S(2)}) collective-permute-start(f32[256,256]{0,1:T(8,128)S(1)} %bitcast.106), channel_id=1, source_target_pairs={{4,0},{6,2},{8,4},{10,6},{12,8},{14,10},{16,12},{18,14},{20,16},{2... | collective-permute-start | bytes 786440 | tf_op jit(solution)/shard_map/ppermute | solution.py:14
  51.3 14.0 %collective-permute-start.4 = (f32[256,256]{0,1:T(8,128)S(1)}, f32[256,256]{0,1:T(8,128)S(1)}, u32[]{:S(2)}, u32[]{:S(2)}) collective-permute-start(f32[256,256]{0,1:T(8,128)S(1)} %bitcast.105), channel_id=1, source_target_pairs={{2,0},{4,2},{6,4},{8,6},{10,8},{12,10},{14,12},{16,14},{18,16},{20... | collective-permute-start | bytes 786440 | tf_op jit(solution)/shard_map/ppermute | solution.py:14
  701.0 1.5 copy-start
Sparse Core Ops, SparseCore 0:
  9.2 228.2 all-gather.8
  239.4 210.7 all-gather.10
  452.0 224.6 all-gather.6
  705.1 54.5 reduce-scatter.1
where the time goes:
time: 770 us; the launch traced here: 769 us
  waiting for transfers between devices  673 us (87%)
  local copies, waits for them, and re-layouts  33.7 us (4%)
  starting transfers between devices  21.4 us (3%)
  matrix products  20.7 us (3%)
  between operations  14.1 us (2%)
    all_gather x1, waiting for transfers between devices, shards(): lax.all_gather(w_query, 'seq', axis=0, tiled=True)  223 us
    all_gather x1, waiting for transfers between devices, shards(): lax.all_gather(value_weight, 'seq', axis=0, tiled=True)  210 us
    all_gather x1, waiting for transfers between devices, shards(): lax.all_gather(key_weight, 'seq', axis=0, tiled=True)  172 us
    reduce_scatter x1, waiting for transfers between devices, shards(): lax.psum_scatter(partial_sum, 'head', scatter_dimension=1, tiled=True)  54.7 us
    unnamed x12, local copies, waits for them, and re-layouts  31.6 us
    ppermute x8, starting transfers between devices, shifted(): return lax.ppermute(array, axis, pairs)  21.3 us
  transfers between devices with their start and end apart: 12, of which 7 were waited for; matrix products, arithmetic and copies ran while one was open for 4% of the time, Pallas kernels for 0%

commit v1 on v0

--- a/solution.py
+++ b/solution.py
@@ -6,6 +6,13 @@
 
 HEAD_SIZE = 128
 WINDOW = 512
+
+
+def cover_region_up(a0, dim_at):
+    current_arr = jnp.concatenate(
+        lax.all_to_all(jnp.stack([a0] * lax.axis_size("seq")), "seq", 0, 0), axis=dim_at
+    )
+    return current_arr
 
 
 def shifted(array, axis, by):
@@ -105,7 +112,7 @@
     q_grad_low = grad_qry.reshape(tok_rows, q_heads * HEAD_SIZE).astype(jnp.bfloat16)
     k_grad_low = key_total.astype(jnp.bfloat16)
     v_grad_low = value_total.astype(jnp.bfloat16)
-    partial_sum = projector(q_grad_low, lax.all_gather(w_query, "seq", axis=0, tiled=True))
+    partial_sum = projector(q_grad_low, cover_region_up(w_query, 0))
     partial_sum = partial_sum + projector(
         k_grad_low, lax.all_gather(key_weight, "seq", axis=0, tiled=True)
     )

time: 770 us -> 658 us (0.85)
  waiting for transfers between devices: 673 us -> 546 us
  starting transfers between devices: 21.4 us -> 34.2 us
    ppermute x8, waiting for transfers between devices: 10.9 us -> 325 us  [shifted(): return lax.ppermute(array, axis, pairs)]
    all_gather x1 -> x0, waiting for transfers between devices: 223 us -> none  [shards(): lax.all_gather(w_query, 'seq', axis=0, tiled=True)]
    all_gather x1, waiting for transfers between devices: 172 us -> 0.02 us  [shards(): lax.all_gather(key_weight, 'seq', axis=0, tiled=True)]
    all_gather x1, waiting for transfers between devices: 210 us -> 166 us  [shards(): lax.all_gather(value_weight, 'seq', axis=0, tiled=True)]
    unnamed x12 -> x23, local copies, waits for them, and re-layouts: 31.6 us -> 9.75 us
    reshape x0 -> x1, local copies, waits for them, and re-layouts: none -> 17.7 us  [cover_region_up(): jnp.concatenate(lax.all_to_all(jnp.stack([a0] * lax.axis_size('seq')), 's...]
    all_to_all x0 -> x1, starting transfers between devices: none -> 15.4 us  [cover_region_up(): lax.all_to_all(jnp.stack([a0] * lax.axis_size('seq')), 'seq', 0, 0)]
  transfers between devices with their start and end apart: 12 -> 12, of which waited for: 7 -> 6; matrix products, arithmetic and copies ran while one was open for 4% -> 4% of each run, Pallas kernels for 0% -> 0%
where the time goes in v1:
time: 658 us; the launch traced here: 657 us
  waiting for transfers between devices  546 us (83%)
  local copies, waits for them, and re-layouts  36.1 us (5%)
  starting transfers between devices  34.2 us (5%)
  matrix products  20.7 us (3%)
  between operations  14.1 us (2%)
    ppermute x8, waiting for transfers between devices, shifted(): return lax.ppermute(array, axis, pairs)  325 us
    all_gather x1, waiting for transfers between devices, shards(): lax.all_gather(value_weight, 'seq', axis=0, tiled=True)  166 us
    reduce_scatter x1, waiting for transfers between devices, shards(): lax.psum_scatter(partial_sum, 'head', scatter_dimension=1, tiled=True)  54.3 us
    ppermute x8, starting transfers between devices, shifted(): return lax.ppermute(array, axis, pairs)  18.6 us
    reshape x1, local copies, waits for them, and re-layouts, cover_region_up(): jnp.concatenate(lax.all_to_all(jnp.stack([a0] * lax.axis_size('seq')), 's...  17.7 us
    all_to_all x1, starting transfers between devices, cover_region_up(): lax.all_to_all(jnp.stack([a0] * lax.axis_size('seq')), 'seq', 0, 0)  15.4 us
  transfers between devices with their start and end apart: 12, of which 6 were waited for; matrix products, arithmetic and copies ran while one was open for 4% of the time, Pallas kernels for 0%

profile of v1, /device:TPU:1, one launch (start us, length us, event | category | flops | bytes accessed | tf_op | source)
XLA Modules:
  0.0 656.6 jit_solution(16018776410200825300)
XLA Ops:
  6.5 7.9 %stack.2 = bf16[128,28,1792]{2,1,0:T(8,128)(2,1)} broadcast(bf16[28,1792]{1,0:T(8,128)(2,1)} %param.17), dimensions={1,2} | broadcast | bytes 12945408 | tf_op jit(solution)/shard_map/stack | solution.py:13
  14.5 15.4 %all-to-all-start = ((bf16[128,28,1792]{2,1,0:T(8,128)(2,1)}), bf16[128,28,1792]{2,1,0:T(8,128)(2,1)}, u32[]{:S(2)}, u32[]{:S(2)}) async-start(bf16[128,28,1792]{2,1,0:T(8,128)(2,1)} %stack.2), calls=%async_computation | async-start | bytes 29360128 | tf_op jit(solution)/shard_map/all_to_all | solution.py:13
  29.9 0.7 all-gather.5.cloned.1.call-update
  30.7 0.1 copy.61
  30.8 3.5 collective-permute-start.3
  34.3 3.1 collective-permute-start.2
  37.4 0.1 copy.54
  37.5 2.3 collective-permute-start.1
  39.8 3.1 collective-permute-start
  43.0 0.0 reduce-scatter.2.cloned.1.call-start
  43.1 0.6 slice.27
  43.7 0.1 copy.57
  43.7 0.1 reduce-window.9
  43.8 0.1 reduce.1
  43.9 0.5 sub.30
  44.4 0.5 copy.64
  45.0 0.5 copy.58
  45.5 1.5 copy.93
  47.6 0.8 select_reduce_fusion
  48.4 0.9 compare_and_fusion
  49.3 0.3 fusion.9
  49.6 314.0 %collective-permute-done.1 = bf16[256,256]{0,1:T(8,128)(2,1)S(1)} collective-permute-done((bf16[256,256]{0,1:T(8,128)(2,1)S(1)}, bf16[256,256]{0,1:T(8,128)(2,1)S(1)}, u32[]{:S(2)}, u32[]{:S(2)}) %collective-permute-start.1) | collective-permute-done | bytes 131104 | tf_op jit(solution)/shard_map/ppermute | solution.py:21
  363.6 1.4 collective-permute-done
  365.0 1.6 fusion.21
  366.7 2.4 fusion.10
  369.1 0.1 fusion.19
  369.2 1.3 collective-permute-start.7
  370.5 1.9 collective-permute-start.6
  372.5 4.0 fusion.2
  376.5 1.9 convolution_bitcast_fusion
  378.4 0.1 fusion.20
  378.4 1.3 collective-permute-start.5
  379.7 2.1 collective-permute-start.4
  381.8 0.9 convolution_convert_fusion
  382.8 0.1 fusion.14
  382.8 8.7 %collective-permute-done.5 = f32[256,256]{0,1:T(8,128)S(1)} collective-permute-done((f32[256,256]{0,1:T(8,128)S(1)}, f32[256,256]{0,1:T(8,128)S(1)}, u32[]{:S(2)}, u32[]{:S(2)}) %collective-permute-start.5) | collective-permute-done | bytes 262176 | tf_op jit(solution)/shard_map/ppermute | solution.py:21
  391.5 1.0 collective-permute-done.4
  392.5 0.1 fusion.16
  392.6 2.5 reshape.145
  395.1 166.0 %all-gather.7.cloned.1.call-done = bf16[128,28,256]{2,1,0:T(8,128)(2,1)} async-done(((bf16[1,28,256]{2,1,0:T(8,128)(2,1)}), bf16[128,28,256]{2,1,0:T(8,128)(2,1)}) %all-gather.7.cloned.1.call-update) | async-done | bytes 1835024 | tf_op jit(solution)/shard_map/all_gather | solution.py:120
  561.1 3.8 reshape.147
  564.9 17.7 %reshape.143 = bf16[3584,1792]{1,0:T(8,128)(2,1)} reshape(bf16[128,28,1792]{2,1,0:T(8,128)(2,1)} %all-to-all-done) | data formatting | bytes 25690112 | tf_op jit(solution)/shard_map/reshape | solution.py:12
  582.5 6.6 %fusion.22 = f32[256,3584]{1,0:T(8,128)S(1)} fusion(bf16[256,1792]{0,1:T(8,128)(2,1)S(1)} %bitcast.100, bf16[3584,1792]{1,0:T(8,128)(2,1)} %reshape.143), kind=kOutput, calls=%fused_computation.35 | convolution fusion | flops 3288334336 | bytes 17432576 | tf_op jit(solution)/shard_map/tc,rc->tr/dot_general | solution.py:62
  589.2 0.7 convolution_add_fusion.1
  589.9 0.8 copy-done
  590.7 2.5 convolution_add_fusion
  593.2 54.3 %reduce-scatter.2.cloned.1.call-done = f32[256,1792]{1,0:T(8,128)} async-done(((f32[256,3584]{1,0:T(8,128)}), f32[256,1792]{1,0:T(8,128)}) %reduce-scatter.2.cloned.1.call-update) | async-done | bytes 1835024 | tf_op jit(solution)/shard_map/reduce_scatter | solution.py:122
  647.6 2.5 convert_element_type.31
  (31 shorter events, 0.3 us)
Async XLA Ops:
  14.4 16.2 %copy-start.3 = (bf16[256,256]{1,0:T(8,128)(2,1)S(1)}, bf16[256,256]{1,0:T(8,128)(2,1)}, u32[]{:S(2)}) copy-start(bf16[256,256]{1,0:T(8,128)(2,1)} %param.12) | copy-start | bytes 393220
  14.4 23.0 %copy-start.4 = (bf16[256,256]{1,0:T(8,128)(2,1)S(1)}, bf16[256,256]{1,0:T(8,128)(2,1)}, u32[]{:S(2)}) copy-start(bf16[256,256]{1,0:T(8,128)(2,1)} %param.11) | copy-start | bytes 393220
  14.4 29.2 %copy-start.5 = (f32[14,256]{1,0:T(8,128)S(1)}, f32[14,256]{1,0:T(8,128)}, u32[]{:S(2)}) copy-start(f32[14,256]{1,0:T(8,128)} %param.15) | copy-start | bytes 43012
  14.4 29.2 %copy-start.7 = (s32[32]{0:T(128)S(1)}, s32[32]{0:T(128)}, u32[]{:S(2)}) copy-start(s32[32]{0:T(128)} %param.16) | copy-start | bytes 388
  14.4 30.0 %copy-start.1 = (bf16[256,1792]{1,0:T(8,128)(2,1)S(1)}, bf16[256,1792]{1,0:T(8,128)(2,1)}, u32[]{:S(2)}) copy-start(bf16[256,1792]{1,0:T(8,128)(2,1)} %param.14) | copy-start | bytes 2752516
  14.5 30.5 %copy-start.2 = (bf16[256,1792]{1,0:T(8,128)(2,1)S(1)}, bf16[256,1792]{1,0:T(8,128)(2,1)}, u32[]{:S(2)}) copy-start(bf16[256,1792]{1,0:T(8,128)(2,1)} %param.10) | copy-start | bytes 2752516
  14.5 550.4 %all-to-all-start = ((bf16[128,28,1792]{2,1,0:T(8,128)(2,1)}), bf16[128,28,1792]{2,1,0:T(8,128)(2,1)}, u32[]{:S(2)}, u32[]{:S(2)}) async-start(bf16[128,28,1792]{2,1,0:T(8,128)(2,1)} %stack.2), calls=%async_computation | async-start | bytes 29360128 | tf_op jit(solution)/shard_map/all_to_all | solution.py:13
  29.9 362.8 %all-gather.5.cloned.1.call-start = ((), (), s32[]{:S(2)}) async-start(), calls=%async_computation.3 | async-start | bytes 2113536 | tf_op jit(solution)/shard_map/all_gather | solution.py:117
  30.6 530.5 %all-gather.7.cloned.1.call-start = ((), (), s32[]{:S(2)}) async-start(), calls=%async_computation.4 | async-start | bytes 2113536 | tf_op jit(solution)/shard_map/all_gather | solution.py:120
  30.8 341.7 %collective-permute-start.3 = (bf16[256,256]{0,1:T(8,128)(2,1)S(1)}, bf16[256,256]{0,1:T(8,128)(2,1)S(1)}, u32[]{:S(2)}, u32[]{:S(2)}) collective-permute-start(bf16[256,256]{0,1:T(8,128)(2,1)S(1)} %copy.61), channel_id=1, source_target_pairs={{0,2},{2,4},{4,6},{6,8},{8,10},{10,12},{12,14},{14,16},{16,18},{18... | collective-permute-start | bytes 393224 | tf_op jit(solution)/shard_map/ppermute | solution.py:21
  34.3 338.1 %collective-permute-start.2 = (bf16[256,256]{0,1:T(8,128)(2,1)S(1)}, bf16[256,256]{0,1:T(8,128)(2,1)S(1)}, u32[]{:S(2)}, u32[]{:S(2)}) collective-permute-start(bf16[256,256]{0,1:T(8,128)(2,1)S(1)} %copy.61), channel_id=1, source_target_pairs={{0,4},{2,6},{4,8},{6,10},{8,12},{10,14},{12,16},{14,18},{16,20},{1... | collective-permute-start | bytes 393224 | tf_op jit(solution)/shard_map/ppermute | solution.py:21
  37.5 326.1 %collective-permute-start.1 = (bf16[256,256]{0,1:T(8,128)(2,1)S(1)}, bf16[256,256]{0,1:T(8,128)(2,1)S(1)}, u32[]{:S(2)}, u32[]{:S(2)}) collective-permute-start(bf16[256,256]{0,1:T(8,128)(2,1)S(1)} %copy.54), channel_id=1, source_target_pairs={{0,2},{2,4},{4,6},{6,8},{8,10},{10,12},{12,14},{14,16},{16,18},{18... | collective-permute-start | bytes 393224 | tf_op jit(solution)/shard_map/ppermute | solution.py:21
  39.8 325.2 %collective-permute-start = (bf16[256,256]{0,1:T(8,128)(2,1)S(1)}, bf16[256,256]{0,1:T(8,128)(2,1)S(1)}, u32[]{:S(2)}, u32[]{:S(2)}) collective-permute-start(bf16[256,256]{0,1:T(8,128)(2,1)S(1)} %copy.54), channel_id=1, source_target_pairs={{0,4},{2,6},{4,8},{6,10},{8,12},{10,14},{12,16},{14,18},{16,20},{1... | collective-permute-start | bytes 393224 | tf_op jit(solution)/shard_map/ppermute | solution.py:21
  43.0 604.6 %reduce-scatter.2.cloned.1.call-start = ((), (), s32[]{:S(2)}) async-start(), calls=%async_computation.2 | async-start | bytes 5505024 | tf_op jit(solution)/shard_map/reduce_scatter | solution.py:122
  43.0 0.6 copy-start.6
  369.2 13.6 %collective-permute-start.7 = (f32[256,256]{0,1:T(8,128)S(1)}, f32[256,256]{0,1:T(8,128)S(1)}, u32[]{:S(2)}, u32[]{:S(2)}) collective-permute-start(f32[256,256]{0,1:T(8,128)S(1)} %bitcast.103), channel_id=1, source_target_pairs={{4,0},{6,2},{8,4},{10,6},{12,8},{14,10},{16,12},{18,14},{20,16},{2... | collective-permute-start | bytes 786440 | tf_op jit(solution)/shard_map/ppermute | solution.py:21
  370.5 12.3 %collective-permute-start.6 = (f32[256,256]{0,1:T(8,128)S(1)}, f32[256,256]{0,1:T(8,128)S(1)}, u32[]{:S(2)}, u32[]{:S(2)}) collective-permute-start(f32[256,256]{0,1:T(8,128)S(1)} %bitcast.102), channel_id=1, source_target_pairs={{2,0},{4,2},{6,4},{8,6},{10,8},{12,10},{14,12},{16,14},{18,16},{20... | collective-permute-start | bytes 786440 | tf_op jit(solution)/shard_map/ppermute | solution.py:21
  378.4 13.1 %collective-permute-start.5 = (f32[256,256]{0,1:T(8,128)S(1)}, f32[256,256]{0,1:T(8,128)S(1)}, u32[]{:S(2)}, u32[]{:S(2)}) collective-permute-start(f32[256,256]{0,1:T(8,128)S(1)} %bitcast.105), channel_id=1, source_target_pairs={{4,0},{6,2},{8,4},{10,6},{12,8},{14,10},{16,12},{18,14},{20,16},{2... | collective-permute-start | bytes 786440 | tf_op jit(solution)/shard_map/ppermute | solution.py:21
  379.7 12.8 %collective-permute-start.4 = (f32[256,256]{0,1:T(8,128)S(1)}, f32[256,256]{0,1:T(8,128)S(1)}, u32[]{:S(2)}, u32[]{:S(2)}) collective-permute-start(f32[256,256]{0,1:T(8,128)S(1)} %bitcast.104), channel_id=1, source_target_pairs={{2,0},{4,2},{6,4},{8,6},{10,8},{12,10},{14,12},{16,14},{18,16},{20... | collective-permute-start | bytes 786440 | tf_op jit(solution)/shard_map/ppermute | solution.py:21
  589.2 1.5 copy-start
Sparse Core Ops, SparseCore 0:
  32.6 276.9 all-gather.4
  311.5 249.6 all-gather.6
  593.4 54.1 reduce-scatter.1
